TPU v7x, 128 devices: a whole 4x4x4 slice. The times are simulated.
128 devices in a mesh: row: 16 (over x, z_hi, core), col: 8 (over z_lo, y).
Axes of the slice: x: 4, y: 4, z: 4 (z_hi: 2, z_lo: 2; z = z_hi * 2 + z_lo), core: 2. Of those that a mesh axis runs over, the one named last changes fastest.
Arguments:
- vectors: bfloat16 [16, 262144], P(None, ('row', 'col'))
- stiffness: bfloat16 [16, 8, 192, 128, 128], P('row', 'col'), may hold values from -0.109375 to 0.109375
- block_row: int32 [16, 8, 192], P('row', 'col'), may hold values from 0 to 127
- block_col: int32 [16, 8, 192], P('row', 'col'), may hold values from 0 to 255
- block_count: int32 [16, 8], P('row', 'col'), may hold values from 1 to 192, as said below
- diag_blocks: bfloat16 [2048, 128, 128], P(('row', 'col'))
- precond: bfloat16 [2048, 128, 128], P(('row', 'col')), may hold values from -0.5 to 0.5
Outputs:
- image: float32 [16, 262144], P(None, ('row', 'col'))
- search: bfloat16 [16, 262144], P(None, ('row', 'col'))
Inputs may be any that keep to these rules, and one draw needn't show every extreme that they name: block_count is at most 192 and equals 192 on at least one grid cell in every draw.
All inputs are finite; a program needn't handle non-finite values.
Results may differ from a plain program's by a relative error of at most 0.0051.
Values may be sent and summed in bfloat16 or wider, within the bound.
No kernel may reach another device: no remote copies, remote signals or barrier semaphores. Data moves between devices by JAX's collectives and lax.ppermute only.
A program may use at most 128 MiB of HBM per device.

v0:
```python
import jax
import jax.numpy as jnp
from jax import lax
from jax.sharding import PartitionSpec as P


def per_device(vectors, stiffness, block_row, block_col, block_count, diag_blocks, precond):
    blocks = stiffness[0, 0]
    rows_index = block_row[0, 0]
    cols_index = block_col[0, 0]
    live_count = block_count[0, 0]
    vec_count = vectors.shape[0]
    owned = diag_blocks.shape[0]
    block_len = diag_blocks.shape[1]
    slots = blocks.shape[0]
    row_devs = lax.axis_size("row")
    col_devs = lax.axis_size("col")
    vectors_f = vectors.astype(jnp.float32)
    lengths_local = jnp.sum(vectors_f * vectors_f, axis=1)
    everything = lax.all_gather(vectors, ("row", "col"), axis=1, tiled=True)
    spread = everything.reshape(vec_count, row_devs, col_devs, owned, block_len)
    row_part = lax.dynamic_index_in_dim(spread, lax.axis_index("row"), 1, False)
    col_part = lax.dynamic_index_in_dim(spread, lax.axis_index("col"), 2, False)
    row_part = row_part.reshape(vec_count, col_devs * owned, block_len)
    col_part = col_part.reshape(vec_count, row_devs * owned, block_len)
    picked_col = jnp.take(col_part, cols_index, axis=1)
    picked_row = jnp.take(row_part, rows_index, axis=1)
    toward_row = jnp.einsum("knb,nab->kna", picked_col, blocks, preferred_element_type=jnp.float32)
    toward_col = jnp.einsum("kna,nab->knb", picked_row, blocks, preferred_element_type=jnp.float32)
    live = jnp.arange(slots, dtype=jnp.int32) < live_count
    row_onehot = (
        (rows_index[None, :] == jnp.arange(col_devs * owned, dtype=jnp.int32)[:, None])
        & live[None, :]
    ).astype(jnp.float32)
    col_onehot = (
        (cols_index[None, :] == jnp.arange(row_devs * owned, dtype=jnp.int32)[:, None])
        & live[None, :]
    ).astype(jnp.float32)
    row_partial = jnp.einsum(
        "kna,gn->kga",
        toward_row,
        row_onehot,
        precision=lax.Precision.HIGHEST,
        preferred_element_type=jnp.float32,
    )
    col_partial = jnp.einsum(
        "kna,gn->kga",
        toward_col,
        col_onehot,
        precision=lax.Precision.HIGHEST,
        preferred_element_type=jnp.float32,
    )
    zero_term = jnp.zeros((vec_count, row_devs, col_devs, owned * block_len), jnp.float32)
    term = lax.dynamic_update_index_in_dim(
        zero_term,
        row_partial.reshape(vec_count, col_devs, owned * block_len),
        lax.axis_index("row"),
        1,
    )
    term = term + lax.dynamic_update_index_in_dim(
        zero_term,
        col_partial.reshape(vec_count, row_devs, owned * block_len),
        lax.axis_index("col"),
        2,
    )
    mine = lax.psum_scatter(
        term.reshape(vec_count, row_devs * col_devs * owned * block_len),
        ("row", "col"),
        scatter_dimension=1,
        tiled=True,
    )
    own_vec = vectors.reshape(vec_count, owned, block_len)
    diag_term = jnp.einsum("nab,knb->kna", diag_blocks, own_vec, preferred_element_type=jnp.float32)
    diag_term = diag_term + jnp.einsum(
        "nba,knb->kna", diag_blocks, own_vec, preferred_element_type=jnp.float32
    )
    image = mine + diag_term.reshape(vec_count, owned * block_len)
    inner_local = jnp.sum(vectors_f * image, axis=1)
    lengths, inner = lax.psum((lengths_local, inner_local), ("row", "col"))
    theta = inner / lengths
    resid = (image - theta[:, None] * vectors_f).astype(jnp.bfloat16)
    search = jnp.einsum(
        "nab,knb->kna",
        precond,
        resid.reshape(vec_count, owned, block_len),
        preferred_element_type=jnp.float32,
    )
    return (image, search.reshape(vec_count, owned * block_len).astype(jnp.bfloat16))


def solution(mesh):
    placed = (
        P(None, ("row", "col")),
        P("row", "col", None, None, None),
        P("row", "col", None),
        P("row", "col", None),
        P("row", "col"),
        P(("row", "col"), None, None),
        P(("row", "col"), None, None),
    )
    return jax.shard_map(
        per_device,
        mesh=mesh,
        in_specs=placed,
        out_specs=(P(None, ("row", "col")), P(None, ("row", "col"))),
        check_vma=False,
    )
```

profile of v0, /device:TPU:1, one launch (start us, length us, event | category | flops | bytes accessed | tf_op | source)
XLA Modules:
  0.0 1170.2 jit_solution(11257969639220290386)
XLA Ops:
  7.2 0.0 copy-start
  7.2 0.0 all-gather.2.cloned.1.call-start
  7.2 0.7 all-gather.2.cloned.1.call-update
  7.9 0.0 reduce-scatter.2.cloned.1.call-start
  8.6 0.7 compare_select_fusion
  9.4 0.7 compare_and_fusion
  10.1 315.9 %all-gather.2.cloned.1.call-done = bf16[16,262144]{1,0:T(8,128)(2,1)} async-done(((bf16[16,2048]{1,0:T(8,128)(2,1)}), bf16[16,262144]{1,0:T(8,128)(2,1)}) %all-gather.2.cloned.1.call-update) | async-done | bytes 8388624 | tf_op jit(solution)/shard_map/all_gather | solution.py:20
  325.9 8.1 copy.31
  334.0 1.1 constant_dynamic-slice_fusion
  335.1 1.5 constant_dynamic-slice_fusion.1
  336.6 0.0 copy-start.4
  336.6 1.7 copy.25
  338.3 0.3 copy.26
  338.7 0.8 gather_fusion.1
  339.4 4.1 fusion
  343.5 0.0 copy-done.4
  343.5 2.9 convolution_bitcast_fusion
  346.5 0.0 copy-start.5
  346.5 1.7 broadcast_in_dim.39
  348.2 2.0 gather_fusion
  350.2 5.5 fusion.2
  355.7 0.0 copy-done.5
  355.7 2.3 fusion.9
  358.0 2.3 broadcast_in_dim.37
  360.3 3.3 copy.15
  363.6 7.9 broadcast_in_dim.34
  371.4 20.5 %dynamic_update_slice.10 = f32[16,16,8,2048]{3,1,0,2:T(8,128)} dynamic-update-slice(f32[16,16,8,2048]{3,1,0,2:T(8,128)} %broadcast_in_dim.34, f32[16,1,8,2048]{3,1,0,2:T(1,128)} %copy.15, s32[]{:T(128)} %constant.42.clone.1, s32[]{:T(128)S(6)} %select_n.55, s32[]{:T(128)} %constant.42.clone.1, s32[]{:T(128)} %constant.42.clone.1) | dynamic-update-slice | bytes 2097156 | tf_op jit(solution)/shard_map/jit(dynamic_update_index_in_dim)/dynamic_update_slice | solution.py:54
  391.9 3.3 add_dynamic-update-slice_fusion
  395.2 15.5 %copy.17 = f32[16,16,8,2048]{3,2,1,0:T(8,128)S(1)} copy(f32[16,16,8,2048]{3,1,0,2:T(8,128)} %add_dynamic-update-slice_fusion) | data formatting | bytes 33554432 | tf_op jit(solution)/shard_map/add | solution.py:60
  410.7 20.1 %copy.32 = f32[2,8,128,2048]{3,1,2,0:T(8,128)} copy(f32[2,8,128,2048]{3,2,1,0:T(8,128)S(1)} %bitcast.82) | data formatting | bytes 33554432
  430.8 0.0 copy-start.1
  430.8 0.0 copy-start.2
  430.8 0.0 reduce-scatter.2.cloned.1.call-update
  430.8 0.0 copy-done
  430.8 0.8 copy-done.1
  431.6 0.4 fusion.38
  432.0 0.3 fusion.12
  432.2 650.6 %reduce-scatter.2.cloned.1.call-done = f32[16,2048]{1,0:T(8,128)} async-done(((f32[16,262144]{1,0:T(8,128)}), f32[16,2048]{1,0:T(8,128)}) %reduce-scatter.2.cloned.1.call-update) | async-done | bytes 131088 | tf_op jit(solution)/shard_map/reduce_scatter | solution.py:66
  1082.9 1.0 fusion.26
  1083.9 0.0 copy-start.3
  1083.9 78.4 %all-reduce = (f32[16]{0:T(128)S(1)}, f32[16]{0:T(128)S(1)}) all-reduce(f32[16]{0:T(128)S(1)} %get-tuple-element.3, f32[16]{0:T(128)S(1)} %get-tuple-element.2), channel_id=1, replica_groups=mesh['row'=16,'col'=8] {'row','col'}, use_global_device_ids=true, to_apply=%region_2.3 | all-reduce | flops 32 | bytes 256 | tf_op jit(solution)/shard_map/psum | solution.py:79
  1162.3 0.0 copy-done.2
  1162.3 0.4 fusion.13
  1162.7 0.7 copy.58
  1163.4 0.0 copy-done.3
  (4 shorter events, 0.0 us)
Async XLA Ops:
  7.2 423.6 %copy-start = (bf16[16,128,128]{2,1,0:T(8,128)(2,1)S(1)}, bf16[16,128,128]{2,1,0:T(8,128)(2,1)}, u32[]{:S(2)}) copy-start(bf16[16,128,128]{2,1,0:T(8,128)(2,1)} %param.12) | copy-start | bytes 1572868
  7.2 318.8 %all-gather.2.cloned.1.call-start = ((), (), s32[]{:S(2)}) async-start(), calls=%async_computation.1 | async-start | bytes 8454144 | tf_op jit(solution)/shard_map/all_gather | solution.py:20
  7.9 1075.0 %reduce-scatter.2.cloned.1.call-start = ((), (), s32[]{:S(2)}) async-start(), calls=%async_computation.2 | async-start | bytes 16908288 | tf_op jit(solution)/shard_map/reduce_scatter | solution.py:66
  336.6 6.9 copy-start.4
  346.5 9.2 copy-start.5
  430.8 0.8 copy-start.1
  430.8 731.5 %copy-start.2 = (bf16[16,128,128]{2,1,0:T(8,128)(2,1)S(1)}, bf16[16,128,128]{2,1,0:T(8,128)(2,1)}, u32[]{:S(2)}) copy-start(bf16[16,128,128]{2,1,0:T(8,128)(2,1)} %param.13) | copy-start | bytes 1572868
  1083.9 79.5 %copy-start.3 = (f32[16,2048]{1,0:T(8,128)}, f32[16,2048]{1,0:T(8,128)S(1)}, u32[]{:S(2)}) copy-start(f32[16,2048]{1,0:T(8,128)S(1)} %get-tuple-element.6) | copy-start | bytes 393220
Sparse Core Ops, SparseCore 0:
  9.7 316.1 all-gather.1
  430.9 651.9 reduce-scatter.1
where the time goes:
time: 1170 us
  waiting for transfers between devices  967 us (83%)
  local copies, waits for them, and re-layouts  88.2 us (8%)
  blocking collectives  78.4 us (7%)
  matrix products  15.8 us (1%)
  between operations  14.8 us (1%)
    reduce_scatter x1, waiting for transfers between devices, per_device(): lax.psum_scatter(term.reshape(vec_count, row_devs * col_devs * owned * bl...  651 us
    all_gather x1, waiting for transfers between devices, per_device(): everything = lax.all_gather(vectors, ('row', 'col'), axis=1, tiled=True)  316 us
    psum x1, blocking collectives, per_device(): lengths, inner = lax.psum((lengths_local, inner_local), ('row', 'col'))  78.4 us
    unnamed x16, local copies, waits for them, and re-layouts  31 us
  transfers between devices with their start and end apart: 2, of which 2 were waited for; matrix products, arithmetic and copies ran while one was open for 0% of the time, Pallas kernels for 0%

commit v1 on v0

--- a/solution.py
+++ b/solution.py
@@ -17,7 +17,10 @@
     col_devs = lax.axis_size("col")
     vectors_f = vectors.astype(jnp.float32)
     lengths_local = jnp.sum(vectors_f * vectors_f, axis=1)
-    everything = lax.all_gather(vectors, ("row", "col"), axis=1, tiled=True)
+    everything = jnp.concatenate(
+        lax.all_to_all(jnp.stack([vectors] * lax.axis_size(("row", "col"))), ("row", "col"), 0, 0),
+        axis=1,
+    )
     spread = everything.reshape(vec_count, row_devs, col_devs, owned, block_len)
     row_part = lax.dynamic_index_in_dim(spread, lax.axis_index("row"), 1, False)
     col_part = lax.dynamic_index_in_dim(spread, lax.axis_index("col"), 2, False)

time: 1170 us -> 981 us (0.84)
  waiting for transfers between devices: 967 us -> 760 us
  starting transfers between devices: 0.08 us -> 12 us
    all_gather x1 -> x0, waiting for transfers between devices: 316 us -> none  [per_device(): everything = lax.all_gather(vectors, ('row', 'col'), axis=1, tiled=True)]
    all_to_all x0 -> x1, waiting for transfers between devices: none -> 105 us  [per_device(): lax.all_to_all(jnp.stack([vectors] * lax.axis_size(('row', 'col'))), ('ro...]
    all_to_all x0 -> x1, starting transfers between devices: none -> 12 us  [per_device(): lax.all_to_all(jnp.stack([vectors] * lax.axis_size(('row', 'col'))), ('ro...]
where the time goes in v1:
time: 981 us; the launch traced here: 980 us
  waiting for transfers between devices  760 us (77%)
  local copies, waits for them, and re-layouts  95.2 us (10%)
  blocking collectives  78.3 us (8%)
  matrix products  15.8 us (2%)
  between operations  14.8 us (2%)
  starting transfers between devices  12 us (1%)
    reduce_scatter x1, waiting for transfers between devices, per_device(): lax.psum_scatter(term.reshape(vec_count, row_devs * col_devs * owned * bl...  655 us
    all_to_all x1, waiting for transfers between devices, per_device(): lax.all_to_all(jnp.stack([vectors] * lax.axis_size(('row', 'col'))), ('ro...  105 us
    psum x1, blocking collectives, per_device(): lengths, inner = lax.psum((lengths_local, inner_local), ('row', 'col'))  78.3 us
    unnamed x16, local copies, waits for them, and re-layouts  31 us
    dynamic_update_slice x1, local copies, waits for them, and re-layouts, per_device(): lax.dynamic_update_index_in_dim(zero_term, row_partial.reshape(vec_count,...  20.4 us
  transfers between devices with their start and end apart: 2, of which 2 were waited for; matrix products, arithmetic and copies ran while one was open for 0% of the time, Pallas kernels for 0%

profile of v1, /device:TPU:1, one launch (start us, length us, event | category | flops | bytes accessed | tf_op | source)
XLA Modules:
  0.0 980.3 jit_solution(263160014986501577)
XLA Ops:
  7.2 0.0 copy-start
  7.2 5.2 stack.2
  12.4 0.0 copy-start.4
  12.4 0.0 copy-start.5
  12.4 12.0 %all-to-all-start = ((bf16[128,16,2048]{2,1,0:T(8,128)(2,1)}), bf16[128,16,2048]{2,1,0:T(8,128)(2,1)}, u32[]{:S(2)}, u32[]{:S(2)}) async-start(bf16[128,16,2048]{2,1,0:T(8,128)(2,1)} %stack.2), calls=%async_computation | async-start | bytes 16777216 | tf_op jit(solution)/shard_map/all_to_all | solution.py:21
  24.3 0.0 reduce-scatter.2.cloned.1.call-start
  25.0 0.0 copy-done.4
  25.1 0.0 copy-done.5
  25.1 105.2 %all-to-all-done = bf16[128,16,2048]{2,1,0:T(8,128)(2,1)} async-done(((bf16[128,16,2048]{2,1,0:T(8,128)(2,1)}), bf16[128,16,2048]{2,1,0:T(8,128)(2,1)}, u32[]{:S(2)}, u32[]{:S(2)}) %all-to-all-start) | async-done | bytes 8388640 | tf_op jit(solution)/shard_map/all_to_all | solution.py:21
  130.4 9.8 copy.54
  140.1 1.1 constant_dynamic-slice_fusion
  141.2 1.4 constant_dynamic-slice_fusion.1
  142.6 0.3 copy.48
  142.9 1.7 copy.36
  144.6 0.3 copy.39
  145.0 0.8 gather_fusion.1
  145.8 4.1 fusion.10
  149.9 2.9 convolution_bitcast_fusion
  152.8 1.7 broadcast_in_dim.39
  154.5 2.0 gather_fusion
  156.5 5.5 fusion.7
  162.0 2.3 fusion.13
  164.3 2.4 broadcast_in_dim.37
  166.6 3.3 copy.38
  169.9 7.9 broadcast_in_dim.34
  177.8 20.4 %dynamic_update_slice.10 = f32[16,16,8,2048]{3,1,0,2:T(8,128)} dynamic-update-slice(f32[16,16,8,2048]{3,1,0,2:T(8,128)} %broadcast_in_dim.34, f32[16,1,8,2048]{3,1,0,2:T(1,128)} %copy.38, s32[]{:T(128)} %constant.42.clone.1, s32[]{:T(128)S(6)} %select_n.55, s32[]{:T(128)} %constant.42.clone.1, s32[]{:T(128)} %constant.42.clone.1) | dynamic-update-slice | bytes 2097156 | tf_op jit(solution)/shard_map/jit(dynamic_update_index_in_dim)/dynamic_update_slice | solution.py:57
  198.1 3.2 add_dynamic-update-slice_fusion
  201.3 15.5 %copy.41 = f32[16,16,8,2048]{3,2,1,0:T(8,128)S(1)} copy(f32[16,16,8,2048]{3,1,0,2:T(8,128)} %add_dynamic-update-slice_fusion) | data formatting | bytes 33554432 | tf_op jit(solution)/shard_map/add | solution.py:63
  216.8 20.1 %copy.55 = f32[2,8,128,2048]{3,1,2,0:T(8,128)} copy(f32[2,8,128,2048]{3,2,1,0:T(8,128)S(1)} %bitcast.86) | data formatting | bytes 33554432
  236.9 0.0 copy-start.1
  236.9 0.0 copy-start.2
  236.9 0.0 reduce-scatter.2.cloned.1.call-update
  236.9 0.0 copy-done
  236.9 0.8 copy-done.1
  237.7 0.4 fusion.42
  238.1 0.3 fusion.16
  238.4 654.7 %reduce-scatter.2.cloned.1.call-done = f32[16,2048]{1,0:T(8,128)} async-done(((f32[16,262144]{1,0:T(8,128)}), f32[16,2048]{1,0:T(8,128)}) %reduce-scatter.2.cloned.1.call-update) | async-done | bytes 131088 | tf_op jit(solution)/shard_map/reduce_scatter | solution.py:69
  893.1 1.0 fusion.30
  894.2 0.0 copy-start.3
  894.2 78.3 %all-reduce = (f32[16]{0:T(128)S(1)}, f32[16]{0:T(128)S(1)}) all-reduce(f32[16]{0:T(128)S(1)} %get-tuple-element.3, f32[16]{0:T(128)S(1)} %get-tuple-element.2), channel_id=1, replica_groups=mesh['row'=16,'col'=8] {'row','col'}, use_global_device_ids=true, to_apply=%region_2.3 | all-reduce | flops 32 | bytes 256 | tf_op jit(solution)/shard_map/psum | solution.py:82
  972.4 0.0 copy-done.2
  972.4 0.4 fusion.17
  972.8 0.7 copy.77
  973.5 0.0 copy-done.3
  (7 shorter events, 0.1 us)
Async XLA Ops:
  7.2 229.8 %copy-start = (bf16[16,128,128]{2,1,0:T(8,128)(2,1)S(1)}, bf16[16,128,128]{2,1,0:T(8,128)(2,1)}, u32[]{:S(2)}) copy-start(bf16[16,128,128]{2,1,0:T(8,128)(2,1)} %param.12) | copy-start | bytes 1572868
  12.4 12.7 %copy-start.4 = (s32[1,1,192]{2,1,0:T(1,128)S(1)}, s32[1,1,192]{2,1,0:T(1,128)}, u32[]{:S(2)}) copy-start(s32[1,1,192]{2,1,0:T(1,128)} %param.10) | copy-start | bytes 2308
  12.4 12.7 %copy-start.5 = (s32[1,1,192]{2,1,0:T(1,128)S(1)}, s32[1,1,192]{2,1,0:T(1,128)}, u32[]{:S(2)}) copy-start(s32[1,1,192]{2,1,0:T(1,128)} %param.9) | copy-start | bytes 2308
  12.4 118.0 %all-to-all-start = ((bf16[128,16,2048]{2,1,0:T(8,128)(2,1)}), bf16[128,16,2048]{2,1,0:T(8,128)(2,1)}, u32[]{:S(2)}, u32[]{:S(2)}) async-start(bf16[128,16,2048]{2,1,0:T(8,128)(2,1)} %stack.2), calls=%async_computation | async-start | bytes 16777216 | tf_op jit(solution)/shard_map/all_to_all | solution.py:21
  24.3 868.8 %reduce-scatter.2.cloned.1.call-start = ((), (), s32[]{:S(2)}) async-start(), calls=%async_computation.2 | async-start | bytes 16908288 | tf_op jit(solution)/shard_map/reduce_scatter | solution.py:69
  236.9 0.8 copy-start.1
  236.9 735.5 %copy-start.2 = (bf16[16,128,128]{2,1,0:T(8,128)(2,1)S(1)}, bf16[16,128,128]{2,1,0:T(8,128)(2,1)}, u32[]{:S(2)}) copy-start(bf16[16,128,128]{2,1,0:T(8,128)(2,1)} %param.13) | copy-start | bytes 1572868
  894.2 79.3 %copy-start.3 = (f32[16,2048]{1,0:T(8,128)}, f32[16,2048]{1,0:T(8,128)S(1)}, u32[]{:S(2)}) copy-start(f32[16,2048]{1,0:T(8,128)S(1)} %get-tuple-element.6) | copy-start | bytes 393220
Sparse Core Ops, SparseCore 0:
  237.1 656.0 reduce-scatter.1

commit v2 on v0

--- a/solution.py
+++ b/solution.py
@@ -76,7 +76,7 @@
     )
     image = mine + diag_term.reshape(vec_count, owned * block_len)
     inner_local = jnp.sum(vectors_f * image, axis=1)
-    lengths, inner = lax.psum((lengths_local, inner_local), ("row", "col"))
+    lengths, inner = lax.psum(lax.psum((lengths_local, inner_local), "col"), "row")
     theta = inner / lengths
     resid = (image - theta[:, None] * vectors_f).astype(jnp.bfloat16)
     search = jnp.einsum(

time: 1170 us -> 1160 us (level)
  blocking collectives: 78.4 us -> 65.2 us
    psum x1 -> x2, blocking collectives: 78.4 us -> 65.2 us  [the longest x1 52.3 us: per_device(): lax.psum(lax.psum((lengths_local, inner_local), 'col'), 'row')]
where the time goes in v2:
time: 1160 us
  waiting for transfers between devices  966 us (83%)
  local copies, waits for them, and re-layouts  88.3 us (8%)
  blocking collectives  65.2 us (6%)
  matrix products  15.8 us (1%)
  between operations  14.8 us (1%)
    reduce_scatter x1, waiting for transfers between devices, per_device(): lax.psum_scatter(term.reshape(vec_count, row_devs * col_devs * owned * bl...  650 us
    all_gather x1, waiting for transfers between devices, per_device(): everything = lax.all_gather(vectors, ('row', 'col'), axis=1, tiled=True)  316 us
    psum x1, blocking collectives, per_device(): lax.psum(lax.psum((lengths_local, inner_local), 'col'), 'row')  52.3 us
    unnamed x16, local copies, waits for them, and re-layouts  31.1 us
  transfers between devices with their start and end apart: 2, of which 2 were waited for; matrix products, arithmetic and copies ran while one was open for 0% of the time, Pallas kernels for 0%

profile of v2, /device:TPU:1, one launch (start us, length us, event | category | flops | bytes accessed | tf_op | source)
XLA Modules:
  0.0 1156.3 jit_solution(209605455334010635)
XLA Ops:
  7.2 0.0 copy-start
  7.2 0.0 all-gather.2.cloned.1.call-start
  7.2 0.7 all-gather.2.cloned.1.call-update
  7.9 0.0 reduce-scatter.2.cloned.1.call-start
  8.6 0.7 compare_select_fusion
  9.4 0.7 compare_and_fusion
  10.1 315.9 %all-gather.2.cloned.1.call-done = bf16[16,262144]{1,0:T(8,128)(2,1)} async-done(((bf16[16,2048]{1,0:T(8,128)(2,1)}), bf16[16,262144]{1,0:T(8,128)(2,1)}) %all-gather.2.cloned.1.call-update) | async-done | bytes 8388624 | tf_op jit(solution)/shard_map/all_gather | solution.py:20
  325.9 8.1 copy.31
  334.0 1.1 constant_dynamic-slice_fusion
  335.1 1.5 constant_dynamic-slice_fusion.1
  336.6 0.0 copy-start.4
  336.6 1.7 copy.25
  338.3 0.3 copy.26
  338.6 0.8 gather_fusion.1
  339.4 4.1 fusion
  343.5 0.0 copy-done.4
  343.5 2.9 convolution_bitcast_fusion
  346.4 0.0 copy-start.5
  346.4 1.7 broadcast_in_dim.39
  348.2 2.0 gather_fusion
  350.2 5.5 fusion.2
  355.6 0.0 copy-done.5
  355.6 2.3 fusion.9
  358.0 2.4 broadcast_in_dim.37
  360.3 3.3 copy.15
  363.6 7.9 broadcast_in_dim.34
  371.4 20.5 %dynamic_update_slice.10 = f32[16,16,8,2048]{3,1,0,2:T(8,128)} dynamic-update-slice(f32[16,16,8,2048]{3,1,0,2:T(8,128)} %broadcast_in_dim.34, f32[16,1,8,2048]{3,1,0,2:T(1,128)} %copy.15, s32[]{:T(128)} %constant.42.clone.1, s32[]{:T(128)S(6)} %select_n.55, s32[]{:T(128)} %constant.42.clone.1, s32[]{:T(128)} %constant.42.clone.1) | dynamic-update-slice | bytes 2097156 | tf_op jit(solution)/shard_map/jit(dynamic_update_index_in_dim)/dynamic_update_slice | solution.py:54
  392.0 3.2 add_dynamic-update-slice_fusion
  395.2 15.5 %copy.17 = f32[16,16,8,2048]{3,2,1,0:T(8,128)S(1)} copy(f32[16,16,8,2048]{3,1,0,2:T(8,128)} %add_dynamic-update-slice_fusion) | data formatting | bytes 33554432 | tf_op jit(solution)/shard_map/add | solution.py:60
  410.7 20.1 %copy.32 = f32[2,8,128,2048]{3,1,2,0:T(8,128)} copy(f32[2,8,128,2048]{3,2,1,0:T(8,128)S(1)} %bitcast.82) | data formatting | bytes 33554432
  430.8 0.0 copy-start.1
  430.8 0.0 copy-start.2
  430.8 0.0 reduce-scatter.2.cloned.1.call-update
  430.8 0.0 copy-done
  430.8 0.8 copy-done.1
  431.6 0.4 fusion.38
  432.0 0.3 fusion.12
  432.2 649.9 %reduce-scatter.2.cloned.1.call-done = f32[16,2048]{1,0:T(8,128)} async-done(((f32[16,262144]{1,0:T(8,128)}), f32[16,2048]{1,0:T(8,128)}) %reduce-scatter.2.cloned.1.call-update) | async-done | bytes 131088 | tf_op jit(solution)/shard_map/reduce_scatter | solution.py:66
  1082.1 1.0 fusion.26
  1083.2 0.0 copy-start.3
  1083.2 12.9 %all-reduce.1 = (f32[16]{0:T(128)S(1)}, f32[16]{0:T(128)S(1)}) all-reduce(f32[16]{0:T(128)S(1)} %get-tuple-element.3, f32[16]{0:T(128)S(1)} %get-tuple-element.2), channel_id=1, replica_groups=mesh['row'=16,'col'=8] {'col'}, use_global_device_ids=true, to_apply=%region_2.3 | all-reduce | flops 32 | bytes 256 | tf_op jit(solution)/shard_map/psum | solution.py:79
  1096.0 52.3 %all-reduce = (f32[16]{0:T(128)S(1)}, f32[16]{0:T(128)S(1)}) all-reduce(f32[16]{0:T(128)S(1)} %get-tuple-element.6, f32[16]{0:T(128)S(1)} %get-tuple-element.7), channel_id=1, replica_groups=mesh['row'=16,'col'=8] {'row'}, use_global_device_ids=true, to_apply=%region_3.4 | all-reduce | flops 32 | bytes 256 | tf_op jit(solution)/shard_map/psum | solution.py:79
  1148.4 0.0 copy-done.2
  1148.4 0.4 fusion.13
  1148.8 0.7 copy.58
  1149.5 0.0 copy-done.3
  (4 shorter events, 0.0 us)
Async XLA Ops:
  7.2 423.6 %copy-start = (bf16[16,128,128]{2,1,0:T(8,128)(2,1)S(1)}, bf16[16,128,128]{2,1,0:T(8,128)(2,1)}, u32[]{:S(2)}) copy-start(bf16[16,128,128]{2,1,0:T(8,128)(2,1)} %param.12) | copy-start | bytes 1572868
  7.2 318.8 %all-gather.2.cloned.1.call-start = ((), (), s32[]{:S(2)}) async-start(), calls=%async_computation.1 | async-start | bytes 8454144 | tf_op jit(solution)/shard_map/all_gather | solution.py:20
  7.9 1074.2 %reduce-scatter.2.cloned.1.call-start = ((), (), s32[]{:S(2)}) async-start(), calls=%async_computation.2 | async-start | bytes 16908288 | tf_op jit(solution)/shard_map/reduce_scatter | solution.py:66
  336.6 6.9 copy-start.4
  346.4 9.2 copy-start.5
  430.8 0.8 copy-start.1
  430.8 717.6 %copy-start.2 = (bf16[16,128,128]{2,1,0:T(8,128)(2,1)S(1)}, bf16[16,128,128]{2,1,0:T(8,128)(2,1)}, u32[]{:S(2)}) copy-start(bf16[16,128,128]{2,1,0:T(8,128)(2,1)} %param.13) | copy-start | bytes 1572868
  1083.2 66.3 %copy-start.3 = (f32[16,2048]{1,0:T(8,128)}, f32[16,2048]{1,0:T(8,128)S(1)}, u32[]{:S(2)}) copy-start(f32[16,2048]{1,0:T(8,128)S(1)} %get-tuple-element.8) | copy-start | bytes 393220
Sparse Core Ops, SparseCore 0:
  9.7 316.1 all-gather.1
  430.9 651.1 reduce-scatter.1
